TPU v7x, 256 devices: a whole 4x4x8 slice. The times are simulated.
256 devices in a mesh: gx: 4 (over x_lo, core), gy: 16 (over x_hi, z), gz: 4 (over y).
Axes of the slice: x: 4 (x_hi: 2, x_lo: 2; x = x_hi * 2 + x_lo), y: 4, z: 8, core: 2. Of those that a mesh axis runs over, the one named last changes fastest.
Arguments:
- field: bfloat16 [64, 8, 384, 1536], P(None, 'gz', 'gy', 'gx'), may hold values from -200 to 200, as said below
- mode_one_factor: bfloat16 [1536, 256], P('gx'), may hold values from -0.15625 to 0.15625
- mode_two_factor: bfloat16 [384, 256], P('gy'), may hold values from -0.3125 to 0.3125
Outputs:
- gram_one: float32 [1536, 1536], P('gx')
- gram_two: float32 [384, 384], P('gy')
- core: bfloat16 [64, 8, 256, 256], P('gx', 'gz', 'gy')
Inputs may be any that keep to these rules, and one draw needn't show every extreme that they name: `field`: the snapshot's values lie within -200 and 200.
All inputs are finite; a program needn't handle non-finite values.
Results may differ from a plain program's by a relative error of at most 0.005.
Values may be sent and summed in bfloat16 or wider, within the bound.
A program may use at most 128 MiB of HBM per device.

v0:
```python
import jax
import jax.numpy as jnp
from jax import lax
from jax.sharding import PartitionSpec as P


def local(field, mode_one_factor, mode_two_factor):
    vars_all, cells_three, cells_two, cells_one = field.shape
    count_gx = lax.axis_size("gx")
    count_gy = lax.axis_size("gy")
    own_rows = vars_all // count_gx
    total_three = cells_three * lax.axis_size("gz")
    total_two = cells_two * count_gy
    rank_one = mode_one_factor.shape[1]
    rank_two = mode_two_factor.shape[1]
    own_ranks = rank_two // count_gy
    factor_one = lax.all_gather(mode_one_factor, "gx", axis=0, tiled=True)
    piece = lax.all_gather(field, "gx", axis=3, tiled=True)
    width = piece.shape[3]
    gram_block = lax.dot_general(
        field.reshape(-1, cells_one),
        piece.reshape(-1, width),
        (((0,), (0,)), ((), ())),
        preferred_element_type=jnp.float32,
    )
    gram_sum = lax.psum(lax.psum(gram_block, "gz"), "gy")
    gram_one = gram_sum * (1.0 / (vars_all * total_three * total_two))
    own_vars = lax.dynamic_slice_in_dim(piece, lax.axis_index("gx") * own_rows, own_rows, axis=0)
    shrunk = (
        jnp.dot(own_vars.reshape(-1, width), factor_one, preferred_element_type=jnp.float32)
        .astype(jnp.bfloat16)
        .reshape(own_rows, cells_three, cells_two, rank_one)
    )
    shrunk_all = lax.all_gather(shrunk, "gy", axis=2, tiled=True)
    gram_two_block = jnp.einsum(
        "akjr,akqr->jq", shrunk, shrunk_all, preferred_element_type=jnp.float32
    )
    gram_two = lax.psum(gram_two_block, ("gx", "gz")) * (1.0 / (vars_all * total_three * rank_one))
    factor_two = lax.all_gather(mode_two_factor, "gy", axis=0, tiled=True)
    own_cols = lax.dynamic_slice_in_dim(
        factor_two, lax.axis_index("gy") * own_ranks, own_ranks, axis=1
    )
    core = jnp.einsum(
        "akjr,js->aksr", shrunk_all, own_cols, preferred_element_type=jnp.float32
    ).astype(jnp.bfloat16)
    return (gram_one, gram_two, core)


def solution(mesh):
    placed = (P(None, "gz", "gy", "gx"), P("gx", None), P("gy", None))
    return jax.shard_map(
        local,
        mesh=mesh,
        in_specs=placed,
        out_specs=(P("gx", None), P("gy", None), P("gx", "gz", "gy", None)),
        check_vma=False,
    )
```

profile of v0, /device:TPU:32, one launch (start us, length us, event | category | flops | bytes accessed | tf_op | source)
XLA Modules:
  0.0 535.0 jit_solution(3255514334234658207)
XLA Ops:
  7.2 0.0 copy-start
  7.2 0.0 all-gather.3.cloned.1.call-start
  7.2 0.7 all-gather.3.cloned.1.call-update
  7.9 0.0 all-reduce.3.cloned.1.call-start
  8.0 95.6 %all-gather.3.cloned.1.call-done = bf16[64,2,24,1536]{3,2,1,0:T(8,128)(2,1)} async-done(((bf16[64,2,24,384]{3,2,1,0:T(8,128)(2,1)}), bf16[64,2,24,1536]{3,2,1,0:T(8,128)(2,1)}) %all-gather.3.cloned.1.call-update) | async-done | bytes 9437200 | tf_op jit(solution)/shard_map/all_gather | solution.py:18
  103.5 7.8 %convolution_bitcast_fusion = f32[384,1536]{1,0:T(8,128)} fusion(bf16[64,2,24,384]{3,2,1,0:T(8,128)(2,1)S(1)} %copy-done, bf16[64,2,24,1536]{3,2,1,0:T(8,128)(2,1)} %all-gather.3.cloned.1.call-done), kind=kOutput, calls=%fused_computation | convolution fusion | flops 3623878656 | bytes 14155776 | tf_op jit(solution)/shard_map/dot_general | solution.py:20
  111.4 0.0 all-reduce.3.cloned.1.call-update
  111.4 0.0 all-reduce.5.cloned.1.call-start
  111.4 70.6 %all-reduce.3.cloned.1.call-done = f32[384,1536]{1,0:T(8,128)} async-done(((f32[384,1536]{1,0:T(8,128)}), f32[384,1536]{1,0:T(8,128)}) %all-reduce.3.cloned.1.call-update) | async-done | bytes 2359312 | tf_op jit(solution)/shard_map/psum | solution.py:26
  182.1 0.0 all-reduce.5.cloned.1.call-update
  182.1 0.0 all-gather.5.cloned.1.call-start
  182.1 8.6 %all_gather.13 = bf16[1536,256]{1,0:T(8,128)(2,1)S(1)} all-gather(bf16[384,256]{1,0:T(8,128)(2,1)S(1)} %copy-done.2), channel_id=1, replica_groups=mesh['gx'=4,'gy'=16,'gz'=4] {'gx'}, dimensions={0}, use_global_device_ids=true | all-gather | bytes 983040 | tf_op jit(solution)/shard_map/all_gather | solution.py:17
  190.7 1.8 constant_dynamic-slice_fusion
  192.5 0.0 copy-start.3
  192.6 1.5 convolution_convert_fusion
  194.1 0.0 all-gather.5.cloned.1.call-update
  194.1 38.6 %all_gather.15 = bf16[384,256]{1,0:T(8,128)(2,1)S(1)} all-gather(bf16[24,256]{1,0:T(8,128)(2,1)S(1)} %copy-done.3), channel_id=1, replica_groups=mesh['gx'=4,'gy'=16,'gz'=4] {'gy'}, dimensions={0}, use_global_device_ids=true | all-gather | bytes 208896 | tf_op jit(solution)/shard_map/all_gather | solution.py:39
  232.8 115.1 %all-reduce.5.cloned.1.call-done = f32[384,1536]{1,0:T(8,128)} async-done(((f32[384,1536]{1,0:T(8,128)}), f32[384,1536]{1,0:T(8,128)}) %all-reduce.5.cloned.1.call-update) | async-done | bytes 2359312 | tf_op jit(solution)/shard_map/psum | solution.py:26
  347.9 3.3 broadcast_multiply_fusion
  351.2 113.4 %all-gather.5.cloned.1.call-done = bf16[16,2,384,256]{3,2,1,0:T(8,128)(2,1)} async-done(((bf16[16,2,24,256]{3,2,1,0:T(8,128)(2,1)}), bf16[16,2,384,256]{3,2,1,0:T(8,128)(2,1)}) %all-gather.5.cloned.1.call-update) | async-done | bytes 6291472 | tf_op jit(solution)/shard_map/all_gather | solution.py:34
  464.6 4.5 convolution_bitcast_fusion.1
  469.1 54.3 %psum.23 = f32[24,384]{1,0:T(8,128)S(1)} all-reduce(f32[24,384]{1,0:T(8,128)S(1)} %convolution_bitcast_fusion.1), channel_id=1, replica_groups=mesh['gx'=4,'gy'=16,'gz'=4] {'gx','gz'}, use_global_device_ids=true, to_apply=%region_2.0 | all-reduce | flops 9216 | bytes 73728 | tf_op jit(solution)/shard_map/psum | solution.py:38
  523.4 0.6 broadcast_multiply_fusion.1
  524.0 4.5 fusion
  (6 shorter events, 0.0 us)
Async XLA Ops:
  7.2 96.4 %copy-start = (bf16[64,2,24,384]{3,2,1,0:T(8,128)(2,1)S(1)}, bf16[64,2,24,384]{3,2,1,0:T(8,128)(2,1)}, u32[]{:S(2)}) copy-start(bf16[64,2,24,384]{3,2,1,0:T(8,128)(2,1)} %param.3) | copy-start | bytes 7077892
  7.2 96.4 %all-gather.3.cloned.1.call-start = ((), (), s32[]{:S(2)}) async-start(), calls=%async_computation | async-start | bytes 11796480 | tf_op jit(solution)/shard_map/all_gather | solution.py:18
  7.9 174.2 %all-reduce.3.cloned.1.call-start = ((), (), s32[]{:S(2)}) async-start(), calls=%async_computation.1 | async-start | bytes 4718592 | tf_op jit(solution)/shard_map/psum | solution.py:26
  111.4 70.8 %copy-start.2 = (bf16[384,256]{1,0:T(8,128)(2,1)S(1)}, bf16[384,256]{1,0:T(8,128)(2,1)}, u32[]{:S(2)}) copy-start(bf16[384,256]{1,0:T(8,128)(2,1)} %param.4) | copy-start | bytes 589828
  111.4 236.5 %all-reduce.5.cloned.1.call-start = ((), (), s32[]{:S(2)}) async-start(), calls=%async_computation.2 | async-start | bytes 4718592 | tf_op jit(solution)/shard_map/psum | solution.py:26
  182.1 282.5 %all-gather.5.cloned.1.call-start = ((), (), s32[]{:S(2)}) async-start(), calls=%async_computation.3 | async-start | bytes 6684672 | tf_op jit(solution)/shard_map/all_gather | solution.py:34
  192.5 1.6 copy-start.3
  232.8 231.8 %copy-start.1 = (bf16[768,256]{1,0:T(8,128)(2,1)S(1)}, bf16[768,256]{1,0:T(8,128)(2,1)}, u32[]{:S(2)}) copy-start(bf16[768,256]{1,0:T(8,128)(2,1)} %convolution_convert_fusion) | copy-start | bytes 1179652
Sparse Core Ops, SparseCore 0:
  9.8 93.6 all-gather.2
  111.5 70.5 all-reduce.2
  184.7 163.1 all-reduce.4
  350.4 114.1 all-gather.4
where the time goes:
time: 535 us
  waiting for transfers between devices  396 us (74%)
  blocking collectives  101 us (19%)
  matrix products  18.3 us (3%)
  between operations  13.8 us (3%)
    psum x2, waiting for transfers between devices, local(): gram_sum = lax.psum(lax.psum(gram_block, 'gz'), 'gy')  186 us
    all_gather x1, waiting for transfers between devices, local(): shrunk_all = lax.all_gather(shrunk, 'gy', axis=2, tiled=True)  113 us
    all_gather x1, waiting for transfers between devices, local(): piece = lax.all_gather(field, 'gx', axis=3, tiled=True)  95.6 us
    psum x1, blocking collectives, local(): lax.psum(gram_two_block, ('gx', 'gz'))  54.3 us
    all_gather x1, blocking collectives, local(): factor_two = lax.all_gather(mode_two_factor, 'gy', axis=0, tiled=True)  38.6 us
  transfers between devices with their start and end apart: 4, of which 4 were waited for; matrix products, arithmetic and copies ran while one was open for 1% of the time, Pallas kernels for 0%

commit v1 on v0

--- a/solution.py
+++ b/solution.py
@@ -31,7 +31,9 @@
         .astype(jnp.bfloat16)
         .reshape(own_rows, cells_three, cells_two, rank_one)
     )
-    shrunk_all = lax.all_gather(shrunk, "gy", axis=2, tiled=True)
+    shrunk_all = jnp.concatenate(
+        lax.all_to_all(jnp.stack([shrunk] * lax.axis_size("gy")), "gy", 0, 0), axis=2
+    )
     gram_two_block = jnp.einsum(
         "akjr,akqr->jq", shrunk, shrunk_all, preferred_element_type=jnp.float32
     )

time: 535 us -> 460 us (0.86)
  waiting for transfers between devices: 396 us -> 236 us
  blocking collectives: 101 us -> 169 us
  starting transfers between devices: 0.16 us -> 10 us
  local copies, waits for them, and re-layouts: 1.83 us -> 11.5 us
    all_gather x1 -> x0, waiting for transfers between devices: 113 us -> none  [local(): shrunk_all = lax.all_gather(shrunk, 'gy', axis=2, tiled=True)]
    all_gather x1, blocking collectives: 38.6 us -> 107 us  [local(): factor_two = lax.all_gather(mode_two_factor, 'gy', axis=0, tiled=True)]
    psum x2, waiting for transfers between devices: 186 us -> 148 us  [local(): gram_sum = lax.psum(lax.psum(gram_block, 'gz'), 'gy')]
    all_to_all x0 -> x1, starting transfers between devices: none -> 9.89 us  [local(): lax.all_to_all(jnp.stack([shrunk] * lax.axis_size('gy')), 'gy', 0, 0)]
    all_gather x1, waiting for transfers between devices: 95.6 us -> 86.9 us  [local(): piece = lax.all_gather(field, 'gx', axis=3, tiled=True)]
  transfers between devices with their start and end apart: 4 -> 4, of which waited for: 4 -> 3; matrix products, arithmetic and copies ran while one was open for 1% -> 2% of each run, Pallas kernels for 0% -> 0%
where the time goes in v1:
time: 460 us; the launch traced here: 459 us
  waiting for transfers between devices  236 us (51%)
  blocking collectives  169 us (37%)
  matrix products  14.8 us (3%)
  between operations  13.8 us (3%)
  local copies, waits for them, and re-layouts  11.5 us (2%)
  starting transfers between devices  10 us (2%)
    psum x2, waiting for transfers between devices, local(): gram_sum = lax.psum(lax.psum(gram_block, 'gz'), 'gy')  148 us
    all_gather x1, blocking collectives, local(): factor_two = lax.all_gather(mode_two_factor, 'gy', axis=0, tiled=True)  107 us
    all_gather x1, waiting for transfers between devices, local(): piece = lax.all_gather(field, 'gx', axis=3, tiled=True)  86.9 us
    psum x1, blocking collectives, local(): lax.psum(gram_two_block, ('gx', 'gz'))  54.3 us
    all_to_all x1, starting transfers between devices, local(): lax.all_to_all(jnp.stack([shrunk] * lax.axis_size('gy')), 'gy', 0, 0)  9.89 us
  transfers between devices with their start and end apart: 4, of which 3 were waited for; matrix products, arithmetic and copies ran while one was open for 2% of the time, Pallas kernels for 0%

profile of v1, /device:TPU:32, one launch (start us, length us, event | category | flops | bytes accessed | tf_op | source)
XLA Modules:
  0.0 459.3 jit_solution(10355961033012015710)
XLA Ops:
  7.2 0.0 all-gather.2.cloned.1.call-start
  7.2 0.7 all-gather.2.cloned.1.call-update
  7.9 0.2 copy-done.2
  8.1 8.6 %all_gather.10 = bf16[1536,256]{1,0:T(8,128)(2,1)S(1)} all-gather(bf16[384,256]{1,0:T(8,128)(2,1)S(1)} %copy-done.2), channel_id=1, replica_groups=mesh['gx'=4,'gy'=16,'gz'=4] {'gx'}, dimensions={0}, use_global_device_ids=true | all-gather | bytes 983040 | tf_op jit(solution)/shard_map/all_gather | solution.py:17
  16.7 86.9 %all-gather.2.cloned.1.call-done = bf16[64,2,24,1536]{3,2,1,0:T(8,128)(2,1)} async-done(((bf16[64,2,24,384]{3,2,1,0:T(8,128)(2,1)}), bf16[64,2,24,1536]{3,2,1,0:T(8,128)(2,1)}) %all-gather.2.cloned.1.call-update) | async-done | bytes 9437200 | tf_op jit(solution)/shard_map/all_gather | solution.py:18
  103.5 1.8 constant_dynamic-slice_fusion
  105.4 0.8 convolution_convert_fusion
  106.1 3.2 stack.3
  109.4 9.9 %all-to-all-start = ((bf16[16,16,2,24,256]{4,3,2,1,0:T(8,128)(2,1)}), bf16[16,16,2,24,256]{4,3,2,1,0:T(8,128)(2,1)}, u32[]{:S(2)}, u32[]{:S(2)}) async-start(bf16[16,16,2,24,256]{4,3,2,1,0:T(8,128)(2,1)} %stack.3), calls=%async_computation | async-start | bytes 12582912 | tf_op jit(solution)/shard_map/all_to_all | solution.py:35
  119.3 0.0 all-reduce.3.cloned.1.call-start
  119.3 7.8 %convolution_bitcast_fusion = f32[384,1536]{1,0:T(8,128)} fusion(bf16[64,2,24,384]{3,2,1,0:T(8,128)(2,1)S(1)} %copy-done.1, bf16[64,2,24,1536]{3,2,1,0:T(8,128)(2,1)} %all-gather.2.cloned.1.call-done), kind=kOutput, calls=%fused_computation | convolution fusion | flops 3623878656 | bytes 14155776 | tf_op jit(solution)/shard_map/dot_general | solution.py:20
  127.1 0.0 all-reduce.3.cloned.1.call-update
  127.2 0.0 all-reduce.5.cloned.1.call-start
  127.2 69.9 %all-reduce.3.cloned.1.call-done = f32[384,1536]{1,0:T(8,128)} async-done(((f32[384,1536]{1,0:T(8,128)}), f32[384,1536]{1,0:T(8,128)}) %all-reduce.3.cloned.1.call-update) | async-done | bytes 2359312 | tf_op jit(solution)/shard_map/psum | solution.py:26
  197.2 0.0 all-reduce.5.cloned.1.call-update
  197.2 106.6 %all_gather.11 = bf16[384,256]{1,0:T(8,128)(2,1)S(1)} all-gather(bf16[24,256]{1,0:T(8,128)(2,1)S(1)} %copy-done.3), channel_id=1, replica_groups=mesh['gx'=4,'gy'=16,'gz'=4] {'gy'}, dimensions={0}, use_global_device_ids=true | all-gather | bytes 208896 | tf_op jit(solution)/shard_map/all_gather | solution.py:41
  303.8 78.3 %all-reduce.5.cloned.1.call-done = f32[384,1536]{1,0:T(8,128)} async-done(((f32[384,1536]{1,0:T(8,128)}), f32[384,1536]{1,0:T(8,128)}) %all-reduce.5.cloned.1.call-update) | async-done | bytes 2359312 | tf_op jit(solution)/shard_map/psum | solution.py:26
  382.1 3.3 broadcast_multiply_fusion
  385.4 3.6 copy.13
  389.0 2.7 copy-done
  391.6 1.7 convolution_bitcast_fusion.1
  393.4 54.3 %psum.23 = f32[24,384]{1,0:T(8,128)S(1)} all-reduce(f32[24,384]{1,0:T(8,128)S(1)} %convolution_bitcast_fusion.1), channel_id=1, replica_groups=mesh['gx'=4,'gy'=16,'gz'=4] {'gx','gz'}, use_global_device_ids=true, to_apply=%region_2.0 | all-reduce | flops 9216 | bytes 73728 | tf_op jit(solution)/shard_map/psum | solution.py:40
  447.6 0.6 broadcast_multiply_fusion.1
  448.3 4.5 fusion
  (7 shorter events, 0.0 us)
Async XLA Ops:
  7.2 0.9 copy-start.2
  7.2 96.4 %all-gather.2.cloned.1.call-start = ((), (), s32[]{:S(2)}) async-start(), calls=%async_computation.1 | async-start | bytes 11796480 | tf_op jit(solution)/shard_map/all_gather | solution.py:18
  109.4 9.9 %copy-start.1 = (bf16[64,2,24,384]{3,2,1,0:T(8,128)(2,1)S(1)}, bf16[64,2,24,384]{3,2,1,0:T(8,128)(2,1)}, u32[]{:S(2)}) copy-start(bf16[64,2,24,384]{3,2,1,0:T(8,128)(2,1)} %param.3) | copy-start | bytes 7077892
  109.4 276.0 %all-to-all-start = ((bf16[16,16,2,24,256]{4,3,2,1,0:T(8,128)(2,1)}), bf16[16,16,2,24,256]{4,3,2,1,0:T(8,128)(2,1)}, u32[]{:S(2)}, u32[]{:S(2)}) async-start(bf16[16,16,2,24,256]{4,3,2,1,0:T(8,128)(2,1)} %stack.3), calls=%async_computation | async-start | bytes 12582912 | tf_op jit(solution)/shard_map/all_to_all | solution.py:35
  119.3 77.9 %all-reduce.3.cloned.1.call-start = ((), (), s32[]{:S(2)}) async-start(), calls=%async_computation.2 | async-start | bytes 4718592 | tf_op jit(solution)/shard_map/psum | solution.py:26
  127.1 70.1 %copy-start.3 = (bf16[24,256]{1,0:T(8,128)(2,1)S(1)}, bf16[24,256]{1,0:T(8,128)(2,1)}, u32[]{:S(2)}) copy-start(bf16[24,256]{1,0:T(8,128)(2,1)} %param.5) | copy-start | bytes 36868
  127.2 254.9 %all-reduce.5.cloned.1.call-start = ((), (), s32[]{:S(2)}) async-start(), calls=%async_computation.3 | async-start | bytes 4718592 | tf_op jit(solution)/shard_map/psum | solution.py:26
  389.0 2.7 copy-start
Sparse Core Ops, SparseCore 0:
  9.8 93.6 all-gather.1
  127.3 69.8 all-reduce.2
  199.8 182.2 all-reduce.4

commit v2 on v0

--- a/solution.py
+++ b/solution.py
@@ -23,7 +23,7 @@
         (((0,), (0,)), ((), ())),
         preferred_element_type=jnp.float32,
     )
-    gram_sum = lax.psum(lax.psum(gram_block, "gz"), "gy")
+    gram_sum = lax.psum(jnp.sum(lax.all_gather(gram_block, "gz"), axis=0), "gy")
     gram_one = gram_sum * (1.0 / (vars_all * total_three * total_two))
     own_vars = lax.dynamic_slice_in_dim(piece, lax.axis_index("gx") * own_rows, own_rows, axis=0)
     shrunk = (

time: 535 us -> 503 us (0.940)
  waiting for transfers between devices: 396 us -> 353 us
  other arithmetic: 3.91 us -> 10.3 us
    psum x2 -> x1, waiting for transfers between devices: 186 us -> 99.6 us  [local(): gram_sum = lax.psum(jnp.sum(lax.all_gather(gram_block, 'gz'), axis=0), 'gy')]
    all_gather x0 -> x1, waiting for transfers between devices: none -> 83.5 us  [local(): gram_sum = lax.psum(jnp.sum(lax.all_gather(gram_block, 'gz'), axis=0), 'gy')]
    all_gather x1, waiting for transfers between devices: 113 us -> 74 us  [local(): shrunk_all = lax.all_gather(shrunk, 'gy', axis=2, tiled=True)]
    reduce_sum x0 -> x1, other arithmetic: none -> 6.37 us  [local(): gram_sum = lax.psum(jnp.sum(lax.all_gather(gram_block, 'gz'), axis=0), 'gy')]
  transfers between devices with their start and end apart: 4 -> 4, of which waited for: 4 -> 4; matrix products, arithmetic and copies ran while one was open for 1% -> 4% of each run, Pallas kernels for 0% -> 0%
where the time goes in v2:
time: 503 us; the launch traced here: 502 us
  waiting for transfers between devices  353 us (70%)
  blocking collectives  102 us (20%)
  matrix products  18.4 us (4%)
  between operations  13.8 us (3%)
  other arithmetic  10.3 us (2%)
    psum x1, waiting for transfers between devices, local(): gram_sum = lax.psum(jnp.sum(lax.all_gather(gram_block, 'gz'), axis=0), 'gy')  99.6 us
    all_gather x1, waiting for transfers between devices, local(): piece = lax.all_gather(field, 'gx', axis=3, tiled=True)  95.6 us
    all_gather x1, waiting for transfers between devices, local(): gram_sum = lax.psum(jnp.sum(lax.all_gather(gram_block, 'gz'), axis=0), 'gy')  83.5 us
    all_gather x1, waiting for transfers between devices, local(): shrunk_all = lax.all_gather(shrunk, 'gy', axis=2, tiled=True)  74 us
    psum x1, blocking collectives, local(): lax.psum(gram_two_block, ('gx', 'gz'))  54.3 us
    all_gather x1, blocking collectives, local(): factor_two = lax.all_gather(mode_two_factor, 'gy', axis=0, tiled=True)  38.8 us
  transfers between devices with their start and end apart: 4, of which 4 were waited for; matrix products, arithmetic and copies ran while one was open for 4% of the time, Pallas kernels for 0%

profile of v2, /device:TPU:32, one launch (start us, length us, event | category | flops | bytes accessed | tf_op | source)
XLA Modules:
  0.0 501.7 jit_solution(6749816770810435192)
XLA Ops:
  7.2 0.0 all-gather.5.cloned.1.call-start
  7.2 0.7 all-gather.5.cloned.1.call-update
  7.9 0.0 all-gather.9.cloned.1.call-start
  8.0 95.6 %all-gather.5.cloned.1.call-done = bf16[64,2,24,1536]{3,2,1,0:T(8,128)(2,1)} async-done(((bf16[64,2,24,384]{3,2,1,0:T(8,128)(2,1)}), bf16[64,2,24,1536]{3,2,1,0:T(8,128)(2,1)}) %all-gather.5.cloned.1.call-update) | async-done | bytes 9437200 | tf_op jit(solution)/shard_map/all_gather | solution.py:18
  103.5 7.8 %convolution_bitcast_fusion = f32[384,1536]{1,0:T(8,128)} fusion(bf16[64,2,24,384]{3,2,1,0:T(8,128)(2,1)S(1)} %copy-done, bf16[64,2,24,1536]{3,2,1,0:T(8,128)(2,1)} %all-gather.5.cloned.1.call-done), kind=kOutput, calls=%fused_computation | convolution fusion | flops 3623878656 | bytes 14155776 | tf_op jit(solution)/shard_map/dot_general | solution.py:20
  111.4 0.0 all-gather.7.cloned.1.call-start
  111.4 0.8 copy-done.2
  112.3 9.3 %all_gather.21 = bf16[1536,256]{1,0:T(8,128)(2,1)S(1)} all-gather(bf16[384,256]{1,0:T(8,128)(2,1)S(1)} %copy-done.2), channel_id=1, replica_groups=mesh['gx'=4,'gy'=16,'gz'=4] {'gx'}, dimensions={0}, use_global_device_ids=true | all-gather | bytes 983040 | tf_op jit(solution)/shard_map/all_gather | solution.py:17
  121.6 1.8 constant_dynamic-slice_fusion
  123.4 1.5 convolution_convert_fusion
  124.9 0.0 all-gather.7.cloned.1.call-update
  124.9 0.0 all-reduce.2.cloned.1.call-start
  125.0 83.5 %all-gather.9.cloned.1.call-done = f32[1536,1536]{1,0:T(8,128)} async-done(((f32[384,1536]{1,0:T(8,128)}), f32[1536,1536]{1,0:T(8,128)}) %all-gather.9.cloned.1.call-update) | async-done | bytes 9437200 | tf_op jit(solution)/shard_map/all_gather | solution.py:26
  208.5 6.4 %reduce_sum.9 = f32[384,1536]{1,0:T(8,128)} reduce(f32[4,384,1536]{2,1,0:T(8,128)} %bitcast.26, f32[]{:T(128)} %constant.4.clone.1), dimensions={0}, to_apply=%region_0.0 | reduce | flops 1769472 | bytes 11796484 | tf_op jit(solution)/shard_map/reduce_sum | solution.py:26
  214.8 0.0 all-reduce.2.cloned.1.call-update
  214.9 0.7 copy-done.3
  215.5 38.8 %all_gather.23 = bf16[384,256]{1,0:T(8,128)(2,1)S(1)} all-gather(bf16[24,256]{1,0:T(8,128)(2,1)S(1)} %copy-done.3), channel_id=1, replica_groups=mesh['gx'=4,'gy'=16,'gz'=4] {'gy'}, dimensions={0}, use_global_device_ids=true | all-gather | bytes 208896 | tf_op jit(solution)/shard_map/all_gather | solution.py:39
  254.4 74.0 %all-gather.7.cloned.1.call-done = bf16[16,2,384,256]{3,2,1,0:T(8,128)(2,1)} async-done(((bf16[16,2,24,256]{3,2,1,0:T(8,128)(2,1)}), bf16[16,2,384,256]{3,2,1,0:T(8,128)(2,1)}) %all-gather.7.cloned.1.call-update) | async-done | bytes 6291472 | tf_op jit(solution)/shard_map/all_gather | solution.py:34
  328.4 4.5 convolution_bitcast_fusion.1
  332.9 54.3 %psum.15 = f32[24,384]{1,0:T(8,128)S(1)} all-reduce(f32[24,384]{1,0:T(8,128)S(1)} %convolution_bitcast_fusion.1), channel_id=1, replica_groups=mesh['gx'=4,'gy'=16,'gz'=4] {'gx','gz'}, use_global_device_ids=true, to_apply=%region_2.0 | all-reduce | flops 9216 | bytes 73728 | tf_op jit(solution)/shard_map/psum | solution.py:38
  387.1 0.6 broadcast_multiply_fusion.1
  387.8 4.6 fusion
  392.3 99.6 %all-reduce.2.cloned.1.call-done = f32[384,1536]{1,0:T(8,128)} async-done(((f32[384,1536]{1,0:T(8,128)}), f32[384,1536]{1,0:T(8,128)}) %all-reduce.2.cloned.1.call-update) | async-done | bytes 2359312 | tf_op jit(solution)/shard_map/psum | solution.py:26
  491.9 3.3 broadcast_multiply_fusion
  (7 shorter events, 0.0 us)
Async XLA Ops:
  7.2 96.4 %copy-start = (bf16[64,2,24,384]{3,2,1,0:T(8,128)(2,1)S(1)}, bf16[64,2,24,384]{3,2,1,0:T(8,128)(2,1)}, u32[]{:S(2)}) copy-start(bf16[64,2,24,384]{3,2,1,0:T(8,128)(2,1)} %param.3) | copy-start | bytes 7077892
  7.2 96.4 %all-gather.5.cloned.1.call-start = ((), (), s32[]{:S(2)}) async-start(), calls=%async_computation | async-start | bytes 11796480 | tf_op jit(solution)/shard_map/all_gather | solution.py:18
  7.9 200.6 %all-gather.9.cloned.1.call-start = ((), (), s32[]{:S(2)}) async-start(), calls=%async_computation.3 | async-start | bytes 11796480 | tf_op jit(solution)/shard_map/all_gather | solution.py:26
  111.4 0.9 copy-start.2
  111.4 217.0 %all-gather.7.cloned.1.call-start = ((), (), s32[]{:S(2)}) async-start(), calls=%async_computation.2 | async-start | bytes 6684672 | tf_op jit(solution)/shard_map/all_gather | solution.py:34
  124.9 367.0 %all-reduce.2.cloned.1.call-start = ((), (), s32[]{:S(2)}) async-start(), calls=%async_computation.1 | async-start | bytes 4718592 | tf_op jit(solution)/shard_map/psum | solution.py:26
  214.8 0.7 copy-start.3
  214.8 113.6 %copy-start.1 = (bf16[768,256]{1,0:T(8,128)(2,1)S(1)}, bf16[768,256]{1,0:T(8,128)(2,1)}, u32[]{:S(2)}) copy-start(bf16[768,256]{1,0:T(8,128)(2,1)} %convolution_convert_fusion) | copy-start | bytes 1179652
Sparse Core Ops, SparseCore 0:
  9.8 93.6 all-gather.4
  111.5 96.9 all-gather.8
  211.1 117.2 all-gather.6
  331.5 160.4 all-reduce.1
